TPU v7x, 32 devices: a whole 2x2x4 slice. The times are simulated.
32 devices in a mesh: dom: 2 (over y), row: 4 (over z), nbr: 4 (over x, core).
Axes of the slice: x: 2, y: 2, z: 4, core: 2. Of those that a mesh axis runs over, the one named last changes fastest.
Arguments:
- blocks: float32 [24, 12, 128, 128], P(('dom', 'row'), 'nbr'), parts along dimension 0, may hold values from -0.15625 to 0.15625
- partner_ids: int32 [24, 12], P(('dom', 'row'), 'nbr'), parts along dimension 0, may hold values from 0 to 11, as said below
- counts: int32 [24], P(('dom', 'row')), parts along dimension 0, may hold values from 1 to 12, as said below
- start: float32 [3072, 32], P(('dom', 'row')), parts along dimension 0, may hold values from -6 to 6
Outputs:
- basis: float32 [3072, 32], P(('dom', 'row')), parts along dimension 0
- ritz: float32 [64, 32], P('dom'), parts along dimension 0
There are 2 independent parts, one for each index of `dom`. A program takes and returns all parts, laid end to end along the dimension named above; each array names one. Nothing has to cross between parts.
Inputs may be any that keep to these rules, and one draw needn't show every extreme that they name: partner_ids[i,0] == i; slots 1 to counts[i] - 1 hold distinct block columns greater than i; slots from counts[i] on hold i. counts[i] <= min(12, 12 - i); counts[0] == 12.
All inputs are finite; a program needn't handle non-finite values.
Results may differ from a plain program's by a relative error of at most 0.0001.
Values sent between devices are 32-bit elements; how exact they have to be, the bound alone decides.
A program may use at most 64 MiB of HBM per device.

v0:
```python
import jax
import jax.numpy as jnp
from jax import lax
from jax.sharding import PartitionSpec as P

ITERS = 2
HIGH = lax.Precision.HIGHEST


def orthonormal(image, gram, total):
    lower = jnp.linalg.cholesky(gram / total)
    return lax.linalg.triangular_solve(lower, image, left_side=False, lower=True, transpose_a=True)


def body(blocks, partner_ids, counts, start):
    block_rows, slots_here = partner_ids.shape
    block_size = blocks.shape[2]
    columns = start.shape[1]
    row_count = lax.axis_size("row")
    all_blocks = block_rows * row_count
    total = all_blocks * block_size
    first_row = lax.axis_index("row") * block_rows
    rows_here = first_row + jnp.arange(block_rows, dtype=jnp.int32)
    slot_index = lax.axis_index("nbr") * slots_here + jnp.arange(slots_here, dtype=jnp.int32)
    valid = slot_index[None, :] < counts[:, None]
    weight = jnp.where(valid, jnp.where(partner_ids == rows_here[:, None], 0.5, 1.0), 0.0).astype(
        jnp.float32
    )
    targets = jnp.concatenate([partner_ids.reshape(-1), rows_here])
    whole = lax.all_gather(start, "row", axis=0, tiled=True)
    cross = jnp.zeros((columns, columns), jnp.float32)
    prior = start
    for step in range(ITERS):
        tiles = whole.reshape(all_blocks, block_size, columns)
        far = tiles[partner_ids] * weight[:, :, None, None]
        near = lax.dynamic_slice_in_dim(tiles, first_row, block_rows, 0)
        direct = jnp.einsum("ipab,ipbk->iak", blocks, far, precision=HIGH)
        transposed = (
            jnp.einsum("ipab,iak->ipbk", blocks, near, precision=HIGH) * weight[:, :, None, None]
        )
        items = jnp.concatenate(
            [transposed.reshape(block_rows * slots_here, block_size, columns), direct], axis=0
        )
        placed = jnp.zeros((all_blocks, block_size, columns), jnp.float32).at[targets].add(items)
        summed = lax.psum_scatter(
            placed.reshape(total, columns), "row", scatter_dimension=0, tiled=True
        )
        image = lax.psum(summed, "nbr")
        gram, cross = lax.psum(
            (jnp.dot(image.T, image, precision=HIGH), jnp.dot(prior.T, image, precision=HIGH)),
            "row",
        )
        cross = cross / total
        prior = orthonormal(image, gram, total)
        if step + 1 < ITERS:
            whole = lax.all_gather(prior, "row", axis=0, tiled=True)
    return (prior, cross)


def solution(mesh):
    return jax.shard_map(
        body,
        mesh=mesh,
        in_specs=(
            P(("dom", "row"), "nbr", None, None),
            P(("dom", "row"), "nbr"),
            P(("dom", "row")),
            P(("dom", "row"), None),
        ),
        out_specs=(P(("dom", "row"), None), P("dom", None)),
        check_vma=False,
    )
```

profile of v0, /device:TPU:0, one launch (start us, length us, event | category | flops | bytes accessed | tf_op | source)
XLA Modules:
  0.0 162.5 jit_solution(3839742283190382437)
XLA Ops:
  7.2 0.0 copy-start
  7.2 0.0 copy-start.1
  7.2 0.0 reduce-scatter.3.cloned.1.call-start
  7.2 0.8 concatenate.32
  8.1 0.0 copy-done.1
  8.1 0.1 reshape.123
  8.2 15.7 %all_gather.6 = f32[1536,32]{0,1:T(8,128)S(1)} all-gather(f32[384,32]{0,1:T(8,128)} %param.10), channel_id=1, replica_groups=mesh['dom'=2,'row'=4,'nbr'=4] {'row'}, dimensions={0}, use_global_device_ids=true | all-gather | bytes 245760 | tf_op jit(solution)/shard_map/all_gather | solution.py:30
  23.9 0.6 gather_fusion
  24.4 0.0 copy-start.2
  24.4 0.6 copy-done.2
  25.1 0.1 select_select_fusion.2
  25.2 0.0 copy-done
  25.2 0.5 convolution_multiply_fusion.1
  25.6 0.8 convolution_bitcast_fusion.3
  26.4 0.1 fusion.16
  26.5 1.1 scatter_fusion
  27.6 0.7 copy_bitcast_fusion.1
  28.3 0.0 reduce-scatter.3.cloned.1.call-update
  28.3 0.0 reduce-scatter.5.cloned.1.call-start
  28.4 21.0 %reduce-scatter.3.cloned.1.call-done = f32[384,32]{0,1:T(8,128)} async-done(((f32[1536,32]{0,1:T(8,128)}), f32[384,32]{0,1:T(8,128)}) %reduce-scatter.3.cloned.1.call-update) | async-done | bytes 49168 | tf_op jit(solution)/shard_map/reduce_scatter | solution.py:45
  49.4 11.0 %psum.35 = f32[384,32]{0,1:T(8,128)S(1)} all-reduce(f32[384,32]{0,1:T(8,128)} %reduce-scatter.3.cloned.1.call-done), channel_id=1, replica_groups=mesh['dom'=2,'row'=4,'nbr'=4] {'nbr'}, use_global_device_ids=true, to_apply=%region_2.3 | all-reduce | flops 12288 | bytes 98304 | tf_op jit(solution)/shard_map/psum | solution.py:48
  60.4 0.2 fusion.20
  60.6 15.9 %psum.36 = f32[32,32]{0,1:T(8,128)S(1)} all-reduce(f32[32,32]{0,1:T(8,128)S(1)} %fusion.20), channel_id=1, replica_groups=mesh['dom'=2,'row'=4,'nbr'=4] {'row'}, use_global_device_ids=true, to_apply=%region_3.4 | all-reduce | flops 1024 | bytes 8192 | tf_op jit(solution)/shard_map/psum | solution.py:49
  76.5 0.1 copy.30
  76.6 2.9 %cholesky.44 = f32[32,32]{1,0:T(8,128)S(1)} custom-call(f32[32,32]{1,0:T(8,128)S(1)} %fusion.13), custom_call_target="Cholesky" | custom-call | tf_op jit(solution)/shard_map/jit(cholesky)/cholesky | solution.py:11
  79.5 0.6 compare_reduce_fusion.1
  80.2 0.7 fusion.8
  80.8 2.4 %custom-call.6 = f32[1,32,32]{1,2,0:T(8,128)S(1)} custom-call(f32[1,32,32]{2,1,0:T(8,128)S(1)} %fusion.8), custom_call_target="InvertDiagBlocksLowerTriangular" | custom-call | tf_op jit(solution)/shard_map/triangular_solve/custom-call.0 | solution.py:12
  83.3 0.3 convolution_bitcast_fusion.2
  83.5 13.6 %all_gather.7 = f32[1536,32]{0,1:T(8,128)S(1)} all-gather(f32[384,32]{0,1:T(8,128)S(1)} %convolution_bitcast_fusion.2), channel_id=1, replica_groups=mesh['dom'=2,'row'=4,'nbr'=4] {'row'}, dimensions={0}, use_global_device_ids=true | all-gather | bytes 245760 | tf_op jit(solution)/shard_map/all_gather | solution.py:56
  97.1 0.6 gather_fusion.1
  97.7 0.5 convolution_multiply_fusion
  98.2 0.8 convolution_bitcast_fusion.1
  99.0 1.1 scatter_fusion.1
  100.1 0.7 copy_bitcast_fusion
  100.8 0.0 reduce-scatter.5.cloned.1.call-update
  100.8 18.8 %reduce-scatter.5.cloned.1.call-done = f32[384,32]{0,1:T(8,128)} async-done(((f32[1536,32]{0,1:T(8,128)}), f32[384,32]{0,1:T(8,128)}) %reduce-scatter.5.cloned.1.call-update) | async-done | bytes 49168 | tf_op jit(solution)/shard_map/reduce_scatter | solution.py:45
  119.6 11.0 %psum.37 = f32[384,32]{0,1:T(8,128)S(1)} all-reduce(f32[384,32]{0,1:T(8,128)} %reduce-scatter.5.cloned.1.call-done), channel_id=1, replica_groups=mesh['dom'=2,'row'=4,'nbr'=4] {'nbr'}, use_global_device_ids=true, to_apply=%region_8.11 | all-reduce | flops 12288 | bytes 98304 | tf_op jit(solution)/shard_map/psum | solution.py:48
  130.6 0.2 fusion.22
  130.8 0.2 fusion.21
  131.0 16.2 %all-reduce = (f32[32,32]{0,1:T(8,128)S(1)}, f32[32,32]{0,1:T(8,128)S(1)}) all-reduce(f32[32,32]{0,1:T(8,128)S(1)} %fusion.21, f32[32,32]{0,1:T(8,128)S(1)} %fusion.22), channel_id=1, replica_groups=mesh['dom'=2,'row'=4,'nbr'=4] {'row'}, use_global_device_ids=true, to_apply=%region_9.12 | all-reduce | flops 2048 | bytes 16384 | tf_op jit(solution)/shard_map/psum | solution.py:49
  147.3 0.7 copy.37
  148.0 0.1 copy.35
  148.0 2.9 %cholesky.55 = f32[32,32]{1,0:T(8,128)S(1)} custom-call(f32[32,32]{1,0:T(8,128)S(1)} %fusion.11), custom_call_target="Cholesky" | custom-call | tf_op jit(solution)/shard_map/jit(cholesky)/cholesky | solution.py:11
  151.0 0.6 compare_reduce_fusion
  151.6 0.7 fusion.9
  152.3 2.4 %custom-call.7 = f32[1,32,32]{1,2,0:T(8,128)S(1)} custom-call(f32[1,32,32]{2,1,0:T(8,128)S(1)} %fusion.9), custom_call_target="InvertDiagBlocksLowerTriangular" | custom-call | tf_op jit(solution)/shard_map/triangular_solve/custom-call.0 | solution.py:12
  154.7 0.9 convolution_bitcast_fusion
  (17 shorter events, 0.2 us)
Async XLA Ops:
  7.2 18.0 %copy-start = (f32[3,3,128,128]{3,2,1,0:T(8,128)S(1)}, f32[3,3,128,128]{3,2,1,0:T(8,128)}, u32[]{:S(2)}) copy-start(f32[3,3,128,128]{3,2,1,0:T(8,128)} %param.7) | copy-start | bytes 1769476
  7.2 0.9 copy-start.1
  7.2 42.2 %reduce-scatter.3.cloned.1.call-start = ((), (), s32[]{:S(2)}) async-start(), calls=%async_computation.2 | async-start | bytes 245760 | tf_op jit(solution)/shard_map/reduce_scatter | solution.py:45
  24.4 0.7 copy-start.2
  28.3 91.3 %reduce-scatter.5.cloned.1.call-start = ((), (), s32[]{:S(2)}) async-start(), calls=%async_computation.3 | async-start | bytes 245760 | tf_op jit(solution)/shard_map/reduce_scatter | solution.py:45
Sparse Core Ops, SparseCore 0:
  28.4 20.9 reduce-scatter.2
  100.9 18.6 reduce-scatter.4
where the time goes:
time: 163 us; the launch traced here: 162 us
  blocking collectives  83.4 us (51%)
  waiting for transfers between devices  39.9 us (24%)
  other arithmetic  15.8 us (10%)
  between operations  14.3 us (9%)
  local copies, waits for them, and re-layouts  4.93 us (3%)
  matrix products  4.18 us (3%)
    reduce_scatter x2, waiting for transfers between devices, body(): lax.psum_scatter(placed.reshape(total, columns), 'row', scatter_dimension...  39.8 us
    psum x2, blocking collectives, body(): lax.psum((jnp.dot(image.T, image, precision=HIGH), jnp.dot(prior.T, image...  32.1 us
    psum x2, blocking collectives, body(): image = lax.psum(summed, 'nbr')  22 us
    all_gather x1, blocking collectives, body(): whole = lax.all_gather(start, 'row', axis=0, tiled=True)  15.7 us
    all_gather x1, blocking collectives, body(): whole = lax.all_gather(prior, 'row', axis=0, tiled=True)  13.6 us
    another operation x6, other arithmetic, orthonormal(): lower = jnp.linalg.cholesky(gram / total)  7.19 us
    another operation x4, other arithmetic, orthonormal(): lax.linalg.triangular_solve(lower, image, left_side=False, lower=True, tr...  6.17 us
  transfers between devices with their start and end apart: 2, of which 2 were waited for; matrix products, arithmetic and copies ran while one was open for 0% of the time, Pallas kernels for 0%

commit v1 on v0

--- a/solution.py
+++ b/solution.py
@@ -2,6 +2,7 @@
 import jax.numpy as jnp
 from jax import lax
 from jax.sharding import PartitionSpec as P
+from jax.lax import all_gather
 
 ITERS = 2
 HIGH = lax.Precision.HIGHEST
@@ -45,7 +46,13 @@
         summed = lax.psum_scatter(
             placed.reshape(total, columns), "row", scatter_dimension=0, tiled=True
         )
-        image = lax.psum(summed, "nbr")
+
+        def post_pipes_now(u, mesh_ax):
+            w2 = all_gather(u, mesh_ax)
+            tile_out = jnp.sum(w2, axis=0)
+            return tile_out
+
+        image = post_pipes_now(summed, "nbr")
         gram, cross = lax.psum(
             (jnp.dot(image.T, image, precision=HIGH), jnp.dot(prior.T, image, precision=HIGH)),
             "row",

time: 163 us -> 152 us (0.933)
  blocking collectives: 83.4 us -> 72.9 us
    psum x2 -> x0, blocking collectives: 22 us -> none  [body(): image = lax.psum(summed, 'nbr')]
    all_gather x0 -> x2, blocking collectives: none -> 11.6 us  [post_pipes_now(): w2 = all_gather(u, mesh_ax)]
where the time goes in v1:
time: 152 us
  blocking collectives  72.9 us (48%)
  waiting for transfers between devices  39.3 us (26%)
  other arithmetic  16.8 us (11%)
  between operations  14.3 us (9%)
  local copies, waits for them, and re-layouts  4.33 us (3%)
  matrix products  4.18 us (3%)
    reduce_scatter x2, waiting for transfers between devices, body(): lax.psum_scatter(placed.reshape(total, columns), 'row', scatter_dimension...  39.3 us
    psum x2, blocking collectives, body(): lax.psum((jnp.dot(image.T, image, precision=HIGH), jnp.dot(prior.T, image...  32 us
    all_gather x1, blocking collectives, body(): whole = lax.all_gather(start, 'row', axis=0, tiled=True)  15.7 us
    all_gather x1, blocking collectives, body(): whole = lax.all_gather(prior, 'row', axis=0, tiled=True)  13.6 us
    all_gather x2, blocking collectives, post_pipes_now(): w2 = all_gather(u, mesh_ax)  11.6 us
    another operation x6, other arithmetic, orthonormal(): lower = jnp.linalg.cholesky(gram / total)  7.19 us
    another operation x4, other arithmetic, orthonormal(): lax.linalg.triangular_solve(lower, image, left_side=False, lower=True, tr...  6.17 us
  transfers between devices with their start and end apart: 2, of which 2 were waited for; matrix products, arithmetic and copies ran while one was open for 0% of the time, Pallas kernels for 0%

profile of v1, /device:TPU:0, one launch (start us, length us, event | category | flops | bytes accessed | tf_op | source)
XLA Modules:
  0.0 151.8 jit_solution(12798288775264183927)
XLA Ops:
  7.2 0.0 copy-start
  7.2 0.0 reduce-scatter.3.cloned.1.call-start
  7.2 0.0 copy-start.1
  7.2 0.7 compare_select_fusion
  8.0 0.0 copy-done.1
  8.0 0.1 concatenate.32
  8.1 15.7 %all_gather.18 = f32[1536,32]{0,1:T(8,128)S(1)} all-gather(f32[384,32]{0,1:T(8,128)} %param.10), channel_id=1, replica_groups=mesh['dom'=2,'row'=4,'nbr'=4] {'row'}, dimensions={0}, use_global_device_ids=true | all-gather | bytes 245760 | tf_op jit(solution)/shard_map/all_gather | solution.py:31
  23.8 0.1 reshape.123
  23.9 0.6 gather_fusion
  24.4 0.0 copy-start.2
  24.4 0.6 copy-done.2
  25.1 0.1 select_select_fusion.2
  25.2 0.0 copy-done
  25.2 0.5 convolution_multiply_fusion.1
  25.6 0.8 convolution_bitcast_fusion.3
  26.4 0.1 fusion.16
  26.5 1.1 scatter_fusion
  27.6 0.7 copy_bitcast_fusion.1
  28.3 0.0 reduce-scatter.3.cloned.1.call-update
  28.3 0.0 reduce-scatter.5.cloned.1.call-start
  28.4 21.0 %reduce-scatter.3.cloned.1.call-done = f32[384,32]{0,1:T(8,128)} async-done(((f32[1536,32]{0,1:T(8,128)}), f32[384,32]{0,1:T(8,128)}) %reduce-scatter.3.cloned.1.call-update) | async-done | bytes 49168 | tf_op jit(solution)/shard_map/reduce_scatter | solution.py:46
  49.4 5.8 %all-gather = f32[1536,32]{0,1:T(8,128)S(1)} all-gather(f32[384,32]{0,1:T(8,128)} %reduce-scatter.3.cloned.1.call-done), channel_id=2, replica_groups=mesh['dom'=2,'row'=4,'nbr'=4] {'nbr'}, dimensions={0}, use_global_device_ids=true | all-gather | bytes 245760 | tf_op jit(solution)/shard_map/all_gather | solution.py:51
  55.2 0.1 reshape.153
  55.3 0.1 reduce_sum.18
  55.4 0.2 fusion.20
  55.6 15.9 %psum.21 = f32[32,32]{0,1:T(8,128)S(1)} all-reduce(f32[32,32]{0,1:T(8,128)S(1)} %fusion.20), channel_id=1, replica_groups=mesh['dom'=2,'row'=4,'nbr'=4] {'row'}, use_global_device_ids=true, to_apply=%region_3.4 | all-reduce | flops 1024 | bytes 8192 | tf_op jit(solution)/shard_map/psum | solution.py:56
  71.4 0.1 copy.42
  71.5 2.9 %cholesky.44 = f32[32,32]{1,0:T(8,128)S(1)} custom-call(f32[32,32]{1,0:T(8,128)S(1)} %fusion.13), custom_call_target="Cholesky" | custom-call | tf_op jit(solution)/shard_map/jit(cholesky)/cholesky | solution.py:12
  74.5 0.6 compare_reduce_fusion.1
  75.1 0.7 fusion.8
  75.8 2.4 %custom-call.6 = f32[1,32,32]{1,2,0:T(8,128)S(1)} custom-call(f32[1,32,32]{2,1,0:T(8,128)S(1)} %fusion.8), custom_call_target="InvertDiagBlocksLowerTriangular" | custom-call | tf_op jit(solution)/shard_map/triangular_solve/custom-call.0 | solution.py:13
  78.2 0.3 convolution_bitcast_fusion.2
  78.5 13.6 %all_gather.21 = f32[1536,32]{0,1:T(8,128)S(1)} all-gather(f32[384,32]{0,1:T(8,128)S(1)} %convolution_bitcast_fusion.2), channel_id=1, replica_groups=mesh['dom'=2,'row'=4,'nbr'=4] {'row'}, dimensions={0}, use_global_device_ids=true | all-gather | bytes 245760 | tf_op jit(solution)/shard_map/all_gather | solution.py:63
  92.1 0.6 gather_fusion.1
  92.6 0.5 convolution_multiply_fusion
  93.1 0.8 convolution_bitcast_fusion.1
  93.9 1.1 scatter_fusion.1
  95.0 0.7 copy_bitcast_fusion
  95.7 0.0 reduce-scatter.5.cloned.1.call-update
  95.7 18.2 %reduce-scatter.5.cloned.1.call-done = f32[384,32]{0,1:T(8,128)} async-done(((f32[1536,32]{0,1:T(8,128)}), f32[384,32]{0,1:T(8,128)}) %reduce-scatter.5.cloned.1.call-update) | async-done | bytes 49168 | tf_op jit(solution)/shard_map/reduce_scatter | solution.py:46
  114.0 5.8 %all-gather.1 = f32[1536,32]{0,1:T(8,128)S(1)} all-gather(f32[384,32]{0,1:T(8,128)} %reduce-scatter.5.cloned.1.call-done), channel_id=3, replica_groups=mesh['dom'=2,'row'=4,'nbr'=4] {'nbr'}, dimensions={0}, use_global_device_ids=true | all-gather | bytes 245760 | tf_op jit(solution)/shard_map/all_gather | solution.py:51
  119.8 0.1 reshape.154
  119.9 0.1 reduce_sum.19
  120.0 0.2 fusion.22
  120.2 0.2 fusion.21
  120.4 16.2 %all-reduce = (f32[32,32]{0,1:T(8,128)S(1)}, f32[32,32]{0,1:T(8,128)S(1)}) all-reduce(f32[32,32]{0,1:T(8,128)S(1)} %fusion.21, f32[32,32]{0,1:T(8,128)S(1)} %fusion.22), channel_id=1, replica_groups=mesh['dom'=2,'row'=4,'nbr'=4] {'row'}, use_global_device_ids=true, to_apply=%region_9.12 | all-reduce | flops 2048 | bytes 16384 | tf_op jit(solution)/shard_map/psum | solution.py:56
  136.6 0.1 copy.47
  136.7 2.9 %cholesky.55 = f32[32,32]{1,0:T(8,128)S(1)} custom-call(f32[32,32]{1,0:T(8,128)S(1)} %fusion.11), custom_call_target="Cholesky" | custom-call | tf_op jit(solution)/shard_map/jit(cholesky)/cholesky | solution.py:12
  139.6 0.6 compare_reduce_fusion
  140.2 0.7 fusion.9
  140.9 2.4 %custom-call.7 = f32[1,32,32]{1,2,0:T(8,128)S(1)} custom-call(f32[1,32,32]{2,1,0:T(8,128)S(1)} %fusion.9), custom_call_target="InvertDiagBlocksLowerTriangular" | custom-call | tf_op jit(solution)/shard_map/triangular_solve/custom-call.0 | solution.py:13
  143.3 0.9 convolution_bitcast_fusion
  144.2 0.7 copy.49
  (16 shorter events, 0.2 us)
Async XLA Ops:
  7.2 18.0 %copy-start = (f32[3,3,128,128]{3,2,1,0:T(8,128)S(1)}, f32[3,3,128,128]{3,2,1,0:T(8,128)}, u32[]{:S(2)}) copy-start(f32[3,3,128,128]{3,2,1,0:T(8,128)} %param.7) | copy-start | bytes 1769476
  7.2 42.2 %reduce-scatter.3.cloned.1.call-start = ((), (), s32[]{:S(2)}) async-start(), calls=%async_computation.2 | async-start | bytes 245760 | tf_op jit(solution)/shard_map/reduce_scatter | solution.py:46
  7.2 0.8 copy-start.1
  24.4 0.7 copy-start.2
  28.3 85.7 %reduce-scatter.5.cloned.1.call-start = ((), (), s32[]{:S(2)}) async-start(), calls=%async_computation.3 | async-start | bytes 245760 | tf_op jit(solution)/shard_map/reduce_scatter | solution.py:46
Sparse Core Ops, SparseCore 0:
  28.5 20.9 reduce-scatter.2
  95.9 18.0 reduce-scatter.4
